TPU v7x, 256 devices: a whole 4x4x8 slice. The times are simulated.
256 devices in a mesh: grp: 8 (over z), blk: 32 (over x, y, core).
Axes of the slice: x: 4, y: 4, z: 8, core: 2. Of those that a mesh axis runs over, the one named last changes fastest.
Arguments:
- tokens: bfloat16 [8, 4096, 1024], P('grp', 'blk'), may hold values from -40 to 40
- lengths: int32 [8, 16], P('grp'), may hold values from 1 to 2176, 4096 in all within a row
- owners: int32 [8], P('grp'), may hold values from 0 to 7
- prefix_cache: bfloat16 [8, 2048, 1024], P('grp', 'blk'), may hold values from -52 to 52
- routes: int32 [8, 4096, 2], P('grp', 'blk'), may hold values from 0 to 7, all different within a row; in each aligned block of 128 rows (0 to 127, 128 to 255, ..., all dimensions but the last counted through in order) at most 40 rows name the same one
- gates: float32 [8, 4096, 2], P('grp', 'blk'), may hold values from 0.2 to 1
- attn_gain: float32 [1024], replicated, may hold values from 0.5 to 1.5
- w_query: bfloat16 [1024, 512], replicated, may hold values from -0.5 to 0.5
- w_keyval: bfloat16 [1024, 1024], replicated, may hold values from -0.1875 to 0.1875
- w_out: bfloat16 [512, 1024], replicated, may hold values from -0.25 to 0.25
- moe_gain: float32 [1024], replicated, may hold values from 0.5 to 1.5
- w_gate: bfloat16 [32, 1024, 704], P('blk'), may hold values from -0.1875 to 0.1875
- w_up: bfloat16 [32, 1024, 704], P('blk'), may hold values from -0.1875 to 0.1875
- w_down: bfloat16 [32, 704, 1024], P('blk'), may hold values from -0.109375 to 0.109375
- final_gain: float32 [1024], replicated, may hold values from 0.5 to 1.5
- unembed: bfloat16 [1024, 32128], P(None, 'blk'), may hold values from -0.5 to 0.5
Outputs:
- hidden: bfloat16 [8, 4096, 1024], P('grp', 'blk')
- suffix_cache: bfloat16 [8, 4096, 1024], P('grp', 'blk')
- request_norm: float32 [8, 16], P('grp')
- greatest: float32 [8, 16], P('grp')
Inputs may be any that keep to these rules, and one draw needn't show every extreme that they name: In each group the lengths sum to 4096, and the longest request has exactly 2176 tokens. `routes`: the two experts of a token differ. Within the 128 rows of one device no expert is named more than 40 times, and in some device's rows an expert is named exactly 40 times.
All inputs are finite; a program needn't handle non-finite values.
Results may differ from a plain program's by a relative error of at most 0.0052.
The roundings to bfloat16 on the way count: a program that leaves them out, or rounds other values in their place, can miss the bound.
Values may be sent and summed in bfloat16 or wider, within the bound.
No kernel may reach another device: no remote copies, remote signals or barrier semaphores. Data moves between devices by JAX's collectives and lax.ppermute only.
A program may use at most 128 MiB of HBM per device.

v0:
```python
import jax
import jax.numpy as jnp
from jax import lax
from jax.sharding import PartitionSpec as P

HEADS = 8
EXPERTS = 8
CAP = 40
epsilon = 1e-06
neg_big = -1e30


def rms_scale(values, gain_vector):
    values = values.astype(jnp.float32)
    return (
        values
        * lax.rsqrt(jnp.mean(values * values, axis=-1, keepdims=True) + epsilon)
        * gain_vector
    )


def request_of(positions, end_points):
    return jnp.sum((positions[:, None] >= end_points[None, :]).astype(jnp.int32), axis=1)


def slot_targets(block_routes):
    flat_routes = block_routes.reshape(-1)
    onehot = (flat_routes[:, None] == jnp.arange(EXPERTS, dtype=jnp.int32)[None, :]).astype(
        jnp.int32
    )
    before = jnp.cumsum(onehot, axis=0) - onehot
    slot_index = jnp.sum(before * onehot, axis=1)
    return (flat_routes * CAP + slot_index).reshape(block_routes.shape)


def dispatch_matrix(targets):
    slot_ids = jnp.arange(EXPERTS * CAP, dtype=jnp.int32)
    matches = (targets[:, 0][None, :] == slot_ids[:, None]) | (
        targets[:, 1][None, :] == slot_ids[:, None]
    )
    return matches.astype(jnp.bfloat16)


def attend_piece(carry_state, query_set, key_part, key_req, key_pos, masked):
    context_sum, row_max, row_total = carry_state
    queries, query_req, query_pos = query_set
    head_count = row_max.shape[0]
    piece_rows = key_part.shape[0]
    attn_width = key_part.shape[1] // 2
    head_size = attn_width // head_count
    key_heads = key_part[:, :attn_width].reshape(piece_rows, head_count, head_size)
    value_heads = key_part[:, attn_width:].reshape(piece_rows, head_count, head_size)
    query_heads = queries.reshape(queries.shape[0], head_count, head_size)
    scores = jnp.einsum(
        "qhd,khd->hqk", query_heads, key_heads, preferred_element_type=jnp.float32
    ) * head_size ** (-0.5)
    if masked:
        allowed = (query_req[:, None] == key_req[None, :]) & (
            key_pos[None, :] <= query_pos[:, None]
        )
        scores = jnp.where(allowed[None], scores, neg_big)
    new_max = jnp.maximum(row_max, jnp.max(scores, axis=-1))
    shrink = jnp.exp(row_max - new_max)
    probs_full = jnp.exp(scores - new_max[..., None])
    row_total = row_total * shrink + jnp.sum(probs_full, axis=-1)
    context_sum = context_sum * shrink[..., None] + jnp.einsum(
        "hqk,khd->hqd",
        probs_full.astype(jnp.bfloat16),
        value_heads,
        preferred_element_type=jnp.float32,
    )
    return (context_sum, new_max, row_total)


def fold_sets(states, query_sets, key_part, key_req, key_pos, masked, request_ends):
    results = []
    for state_one, set_one in zip(states, query_sets):
        if masked:
            first_req = set_one[1][0]
            earliest = jnp.where(first_req > 0, request_ends[jnp.maximum(first_req - 1, 0)], 0)
            needed = (key_pos[0] >= 0) & (key_pos[0] <= set_one[2][-1]) & (key_pos[-1] >= earliest)
            results.append(
                lax.cond(
                    needed,
                    lambda carried: attend_piece(
                        carried, set_one, key_part, key_req, key_pos, True
                    ),
                    lambda carried: carried,
                    state_one,
                )
            )
        else:
            results.append(attend_piece(state_one, set_one, key_part, key_req, key_pos, False))
    return tuple(results)


def empty_state(query_count, head_count, head_size):
    return (
        jnp.zeros((head_count, query_count, head_size), jnp.float32),
        jnp.full((head_count, query_count), neg_big, jnp.float32),
        jnp.zeros((head_count, query_count), jnp.float32),
    )


def finish_context(state_one):
    context_sum, row_max, row_total = state_one
    context = context_sum / row_total[..., None]
    return jnp.transpose(context, (1, 0, 2)).reshape(context.shape[1], -1).astype(jnp.bfloat16)


def local(
    tokens,
    lengths,
    owners,
    prefix_cache,
    routes,
    gates,
    attn_gain,
    w_query,
    w_keyval,
    w_out,
    moe_gain,
    w_gate,
    w_up,
    w_down,
    final_gain,
    unembed,
):
    tok_rows = tokens.shape[1]
    model_width = tokens.shape[2]
    head_count = HEADS
    head_size = w_query.shape[1] // head_count
    blocks = lax.axis_size("blk")
    block_index = lax.axis_index("blk")
    stream = tokens[0]
    normed = rms_scale(stream, attn_gain).astype(jnp.bfloat16)
    queries = jnp.dot(normed, w_query, preferred_element_type=jnp.float32).astype(jnp.bfloat16)
    suffix_kv = jnp.dot(normed, w_keyval, preferred_element_type=jnp.float32).astype(jnp.bfloat16)
    request_ends = jnp.cumsum(lengths[0])
    positions = block_index * tok_rows + jnp.arange(tok_rows, dtype=jnp.int32)
    requests = request_of(positions, request_ends)
    query_sets = ((queries, requests, positions),)
    states = tuple((empty_state(one[0].shape[0], head_count, head_size) for one in query_sets))
    owner_id = owners[0]
    blank_prefix = jnp.zeros_like(prefix_cache[0])
    arrived = lax.all_gather(prefix_cache, "grp", axis=0, tiled=True)
    first_row = jnp.int32(0)
    shard_count = arrived.shape[0]
    inside = (owner_id >= first_row) & (owner_id < first_row + shard_count)
    offset = jnp.clip(owner_id, 0, shard_count - 1)
    owner_prefix = jnp.where(
        inside, lax.dynamic_index_in_dim(arrived, offset, 0, keepdims=False), blank_prefix
    )
    states = fold_sets(
        states,
        query_sets,
        lax.all_gather(owner_prefix, "blk", axis=0, tiled=True),
        None,
        None,
        False,
        request_ends,
    )
    arrived = lax.all_gather(suffix_kv, "blk", axis=0, tiled=True)
    key_pos = jnp.arange(arrived.shape[0], dtype=jnp.int32)
    states = fold_sets(
        states, query_sets, arrived, request_of(key_pos, request_ends), key_pos, True, request_ends
    )
    contexts = [finish_context(one) for one in states]
    context = contexts[0]
    mixed_stream = stream.astype(jnp.float32) + jnp.dot(
        context, w_out, preferred_element_type=jnp.float32
    )
    routed_in = rms_scale(mixed_stream, moe_gain).astype(jnp.bfloat16)
    targets = slot_targets(routes[0])
    dispatch = dispatch_matrix(targets)
    packed = jnp.dot(dispatch, routed_in, preferred_element_type=jnp.float32).astype(jnp.bfloat16)
    split_count = blocks // EXPERTS
    outgoing = jnp.broadcast_to(
        packed.reshape(EXPERTS, 1, CAP, model_width), (EXPERTS, split_count, CAP, model_width)
    ).reshape(blocks, CAP, model_width)
    arrived = lax.all_to_all(outgoing, "blk", split_axis=0, concat_axis=0, tiled=True)
    flat_rows = arrived.reshape(-1, model_width)
    gate_value = jnp.dot(flat_rows, w_gate[0], preferred_element_type=jnp.float32)
    up_value = jnp.dot(flat_rows, w_up[0], preferred_element_type=jnp.float32)
    hidden = (jax.nn.gelu(gate_value, approximate=True) * up_value).astype(jnp.bfloat16)
    partial_value = (
        jnp.dot(hidden, w_down[0], preferred_element_type=jnp.float32)
        .astype(jnp.bfloat16)
        .reshape(arrived.shape)
    )
    returned_parts = lax.all_to_all(partial_value, "blk", split_axis=0, concat_axis=0, tiled=True)
    summed = jnp.sum(
        returned_parts.reshape(EXPERTS, split_count, CAP, model_width).astype(jnp.float32), axis=1
    ).reshape(EXPERTS * CAP, model_width)
    first_pick = jnp.take(summed, targets[:, 0], axis=0)
    second_pick = jnp.take(summed, targets[:, 1], axis=0)
    moe_out = gates[0][:, 0:1] * first_pick + gates[0][:, 1:2] * second_pick
    hidden_out = (mixed_stream + moe_out).astype(jnp.bfloat16)
    squares = jnp.sum(jnp.square(hidden_out.astype(jnp.float32)), axis=1)
    member = requests[:, None] == jnp.arange(lengths.shape[1], dtype=jnp.int32)[None, :]
    norm_terms = jnp.sum(jnp.where(member, squares[:, None], 0.0), axis=0)
    is_last = positions[:, None] == (request_ends - 1)[None, :]
    final_rows = rms_scale(hidden_out, final_gain).astype(jnp.bfloat16)
    last_terms = jnp.einsum(
        "tr,td->rd", is_last.astype(jnp.bfloat16), final_rows, preferred_element_type=jnp.float32
    )
    norm_sums, last_rows = (
        lax.psum(norm_terms.astype(jnp.bfloat16), "blk").astype(jnp.float32),
        lax.psum(last_terms.astype(jnp.bfloat16), "blk").astype(jnp.float32),
    )
    logits = jnp.dot(last_rows.astype(jnp.bfloat16), unembed, preferred_element_type=jnp.float32)
    greatest = lax.pmax(jnp.max(logits, axis=1), "blk")
    request_norm = jnp.sqrt(norm_sums / (lengths[0].astype(jnp.float32) * model_width))
    return (hidden_out[None], suffix_kv[None], request_norm[None], greatest[None])


def solution(mesh):
    placed = (
        P("grp", "blk", None),
        P("grp", None),
        P("grp"),
        P("grp", "blk", None),
        P("grp", "blk", None),
        P("grp", "blk", None),
        P(),
        P(),
        P(),
        P(),
        P(),
        P("blk", None, None),
        P("blk", None, None),
        P("blk", None, None),
        P(),
        P(None, "blk"),
    )
    return jax.shard_map(
        local,
        mesh=mesh,
        in_specs=placed,
        out_specs=(P("grp", "blk", None), P("grp", "blk", None), P("grp", None), P("grp", None)),
        check_vma=False,
    )
```

profile of v0, /device:TPU:1, one launch (start us, length us, event | category | flops | bytes accessed | tf_op | source)
XLA Modules:
  0.0 506.1 jit_solution(9666139919563082497)
XLA Ops:
  8.9 38.4 %all-gather.5.cloned.1.call-done = bf16[8,64,1024]{2,1,0:T(8,128)(2,1)} async-done(((bf16[1,64,1024]{2,1,0:T(8,128)(2,1)}), bf16[8,64,1024]{2,1,0:T(8,128)(2,1)}) %all-gather.5.cloned.1.call-update) | async-done | bytes 1048592 | tf_op jit(solution)/shard_map/all_gather | solution.py:146
  50.1 2.2 convolution_convert_fusion.2
  57.5 48.1 %all-gather.9.cloned.1.call-done = bf16[1,2048,1024]{2,1,0:T(8,128)(2,1)} async-done(((bf16[1,64,1024]{2,1,0:T(8,128)(2,1)}), bf16[1,2048,1024]{2,1,0:T(8,128)(2,1)}) %all-gather.9.cloned.1.call-update) | async-done | bytes 4194320 | tf_op jit(solution)/shard_map/all_gather | solution.py:157
  105.6 3.8 fusion.69
  109.4 2.5 copy.56
  111.9 2.9 copy.55
  117.9 1.9 fusion.29
  119.7 46.3 %all-gather.7.cloned.1.call-done = bf16[4096,1024]{1,0:T(8,128)(2,1)} async-done(((bf16[128,1024]{1,0:T(8,128)(2,1)}), bf16[4096,1024]{1,0:T(8,128)(2,1)}) %all-gather.7.cloned.1.call-update) | async-done | bytes 8388624 | tf_op jit(solution)/shard_map/all_gather | solution.py:163
  166.1 40.8 %conditional.1 = ((f32[8,128,64]{1,2,0:T(8,128)S(1)}, f32[8,128]{1,0:T(8,128)S(1)})) conditional(s32[]{:T(128)} %convert_element_type.95, (f32[8,128,64]{1,2,0:T(8,128)S(1)}, f32[8,128]{1,0:T(8,128)S(1)}) %tuple.16, (s32[128]{0:T(128)S(1)}, s32[4096,16]{0,1:T(8,128)S(1)}, s32[4096]{0:T(1024)S(1)}, s32[128]{0:T(128)S(1)}, ...), branch_computations={%region_5.6_spmd, %region_6.10_spmd} | conditional | flops 1121646592 | bytes 162767936 | solution.py:83
  166.3 11.4 %copy.58 = bf16[4096,1024]{0,1:T(8,128)(2,1)} copy(bf16[4096,1024]{1,0:T(8,128)(2,1)} %get-tuple-element.83) | data formatting | bytes 16777216 | tf_op jit(solution)/shard_map
  177.7 6.1 %fusion.68 = (bf16[4096,512]{0,1:T(8,128)(2,1)}, bf16[4096,512]{0,1:T(8,128)(2,1)}) fusion(bf16[4096,1024]{0,1:T(8,128)(2,1)} %copy.58), kind=kLoop, calls=%fused_computation.115 | loop fusion | bytes 16777216 | tf_op jit(solution)/shard_map/cond/branch_1_fun/slice | solution.py:51
  184.4 5.0 fusion
  189.4 4.8 fusion.1
  195.1 11.7 %fusion.6 = f32[8,128,64]{1,2,0:T(8,128)S(1)} fusion(bf16[4096,8,64]{0,2,1:T(8,128)(2,1)} %bitcast.90, f32[8,128,4096]{2,1,0:T(8,128)} %copy-done.2, f32[8,128]{1,0:T(8,128)S(1)} %max.12, pred[128,4096]{1,0:T(8,128)(4,1)S(1)} %compare_and_fusion, f32[8,128,64]{1,2,0:T(8,128)S(1)} %get-tuple-element.25, f32[8,128]{1,0:T(8,128)S(1)} %get-tuple-element.92), kind=kOutput, calls=%fused_computation.10 | convolution fusion | flops 553779200 | bytes 22028288 | tf_op jit(solution)/shard_map/cond/branch_1_fun/hqk,khd->hqd/dot_general | solution.py:66
  208.1 39.5 %all_to_all.10 = bf16[32,40,1024]{2,1,0:T(8,128)(2,1)S(1)} all-to-all(bf16[32,40,1024]{2,1,0:T(8,128)(2,1)S(1)} %bitcast.86), channel_id=1, replica_groups=mesh['grp'=8,'blk'=32] {'blk'}, dimensions={0} | all-to-all | bytes 5242880 | tf_op jit(solution)/shard_map/all_to_all | solution.py:181
  249.2 3.8 fusion.27
  253.0 9.7 %convolution_convert_fusion = bf16[1280,1024]{1,0:T(8,128)(2,1)} fusion(bf16[1,704,1024]{2,1,0:T(8,128)(2,1)S(1)} %copy-done.20, bf16[1280,1024]{1,0:T(8,128)(2,1)} %bitcast.93, f32[1280,704]{0,1:T(8,128)} %fusion.27, bf16[1,1024,704]{1,2,0:T(8,128)(2,1)} %param.32), kind=kOutput, calls=%fused_computation.25 | convolution fusion | flops 3701309440 | bytes 11730944 | tf_op jit(solution)/shard_map/dot_general | solution.py:187
  262.8 4.7 all-to-all-start.1
  267.6 33.5 %all-to-all-done.1 = bf16[32,40,1024]{2,1,0:T(8,128)(2,1)} async-done(((bf16[32,40,1024]{2,1,0:T(8,128)(2,1)}), bf16[32,40,1024]{2,1,0:T(8,128)(2,1)}, u32[]{:S(2)}, u32[]{:S(2)}) %all-to-all-start.1) | async-done | bytes 2621472 | tf_op jit(solution)/shard_map/all_to_all | solution.py:191
  301.1 2.4 convert_reduce_fusion
  306.6 1.7 fusion.34
  308.7 119.8 %all-reduce = (bf16[16]{0:T(256)(128)(2,1)S(1)}, bf16[16,1024]{1,0:T(8,128)(2,1)S(1)}) all-reduce(bf16[16]{0:T(256)(128)(2,1)S(1)} %select_reduce_fusion, bf16[16,1024]{1,0:T(8,128)(2,1)S(1)} %convolution_convert_fusion.4), channel_id=1, replica_groups=mesh['grp'=8,'blk'=32] {'blk'}, use_global_device_ids=true, to_apply=%region_17.19 | all-reduce | flops 16400 | bytes 65600 | tf_op jit(solution)/shard_map/psum | solution.py:208
  429.0 2.3 convolution_reduce_fusion
  431.4 68.2 %pmax.7 = f32[1,16]{1,0:T(1,128)} all-reduce(f32[1,16]{1,0:T(1,128)S(1)} %bitcast.101), channel_id=1, replica_groups=mesh['grp'=8,'blk'=32] {'blk'}, use_global_device_ids=true, to_apply=%region_20.22 | all-reduce | flops 16 | bytes 128 | tf_op jit(solution)/shard_map/pmax | solution.py:212
  (104 shorter events, 18.7 us)
Async XLA Ops:
  7.2 42.9 %copy-start = (bf16[1024,1024]{1,0:T(8,128)(2,1)S(1)}, bf16[1024,1024]{1,0:T(8,128)(2,1)}, u32[]{:S(2)}) copy-start(bf16[1024,1024]{1,0:T(8,128)(2,1)} %param.28) | copy-start | bytes 6291460
  7.2 48.3 %copy-start.5 = (bf16[1,128,1024]{2,1,0:T(8,128)(2,1)S(1)}, bf16[1,128,1024]{2,1,0:T(8,128)(2,1)}, u32[]{:S(2)}) copy-start(bf16[1,128,1024]{2,1,0:T(8,128)(2,1)} %param.20) | copy-start | bytes 786436
  7.2 48.3 %copy-start.10 = (f32[1024]{0:T(1024)S(1)}, f32[1024]{0:T(1024)}, u32[]{:S(2)}) copy-start(f32[1024]{0:T(1024)} %param.26) | copy-start | bytes 12292
  7.2 45.0 %copy-start.12 = (s32[1,128,2]{1,2,0:T(2,128)S(1)}, s32[1,128,2]{1,2,0:T(2,128)}, u32[]{:S(2)}) copy-start(s32[1,128,2]{1,2,0:T(2,128)} %param.24) | copy-start | bytes 3076
  7.2 46.7 %copy-start.14 = (s32[1,16]{1,0:T(1,128)S(1)}, s32[1,16]{1,0:T(1,128)}, u32[]{:S(2)}) copy-start(s32[1,16]{1,0:T(1,128)} %param.21) | copy-start | bytes 196
  7.2 48.3 %copy-start.7 = (bf16[1024,512]{1,0:T(8,128)(2,1)S(1)}, bf16[1024,512]{1,0:T(8,128)(2,1)}, u32[]{:S(2)}) copy-start(bf16[1024,512]{1,0:T(8,128)(2,1)} %param.27) | copy-start | bytes 3145732
  7.2 40.1 %all-gather.5.cloned.1.call-start = ((), (), s32[]{:S(2)}) async-start(), calls=%async_computation.2 | async-start | bytes 1179648 | tf_op jit(solution)/shard_map/all_gather | solution.py:146
  8.0 97.6 %all-gather.9.cloned.1.call-start = ((), (), s32[]{:S(2)}) async-start(), calls=%async_computation.4 | async-start | bytes 4325376 | tf_op jit(solution)/shard_map/all_gather | solution.py:157
  48.9 117.2 %all-gather.7.cloned.1.call-start = ((), (), s32[]{:S(2)}) async-start(), calls=%async_computation.3 | async-start | bytes 8650752 | tf_op jit(solution)/shard_map/all_gather | solution.py:163
  52.7 3.4 copy-start.15
  116.2 1.7 copy-start.3
  117.9 48.2 %copy-start.16 = (s32[128]{0:T(128)S(1)}, s32[128]{0:T(128)}, u32[]{:S(2)}) copy-start(s32[128]{0:T(128)} %copy-done.15) | copy-start | bytes 1540
  117.9 48.2 %copy-start.18 = (s32[128]{0:T(128)S(1)}, s32[128]{0:T(128)}, u32[]{:S(2)}) copy-start(s32[128]{0:T(128)} %copy-done.17) | copy-start | bytes 1540
  166.1 40.8 %copy-start.8 = (bf16[512,1024]{1,0:T(8,128)(2,1)S(1)}, bf16[512,1024]{1,0:T(8,128)(2,1)}, u32[]{:S(2)}) copy-start(bf16[512,1024]{1,0:T(8,128)(2,1)} %param.29) | copy-start | bytes 3145732
  166.1 41.3 %copy-start.11 = (f32[1024]{0:T(1024)S(1)}, f32[1024]{0:T(1024)}, u32[]{:S(2)}) copy-start(f32[1024]{0:T(1024)} %param.30) | copy-start | bytes 12292
  189.4 5.7 %copy-start.2 = (f32[8,128,4096]{2,1,0:T(8,128)}, f32[8,128,4096]{2,1,0:T(8,128)S(1)}, u32[]{:S(2)}) copy-start(f32[8,128,4096]{2,1,0:T(8,128)S(1)} %get-tuple-element.98) | copy-start | bytes 50331652 | tf_op jit(solution)/shard_map/cond
  207.3 40.3 %copy-start.4 = (f32[128,1024]{1,0:T(8,128)}, f32[128,1024]{1,0:T(8,128)S(1)}, u32[]{:S(2)}) copy-start(f32[128,1024]{1,0:T(8,128)S(1)} %get-tuple-element.108) | copy-start | bytes 1572868
  207.8 41.4 %copy-start.19 = (bf16[1,1024,704]{1,2,0:T(8,128)(2,1)S(1)}, bf16[1,1024,704]{1,2,0:T(8,128)(2,1)}, u32[]{:S(2)}) copy-start(bf16[1,1024,704]{1,2,0:T(8,128)(2,1)} %param.31) | copy-start | bytes 4325380
  249.2 3.8 copy-start.20
  262.8 4.8 copy-start.13
  262.8 38.3 %all-to-all-start.1 = ((bf16[32,40,1024]{2,1,0:T(8,128)(2,1)}), bf16[32,40,1024]{2,1,0:T(8,128)(2,1)}, u32[]{:S(2)}, u32[]{:S(2)}) async-start(bf16[32,40,1024]{2,1,0:T(8,128)(2,1)} %bitcast.91), calls=%async_computation.1 | async-start | bytes 5242880 | tf_op jit(solution)/shard_map/all_to_all | solution.py:191
  303.5 196.1 %copy-start.1 = (bf16[1024,1024]{1,0:T(8,128)(2,1)S(1)}, bf16[1024,1024]{1,0:T(8,128)(2,1)}, u32[]{:S(2)}) copy-start(bf16[1024,1024]{1,0:T(8,128)(2,1)} %param.28) | copy-start | bytes 6291460
  305.0 3.3 copy-start.21
  308.3 191.2 %copy-start.9 = (bf16[128,1024]{1,0:T(8,128)(2,1)}, bf16[128,1024]{1,0:T(8,128)(2,1)S(1)}, u32[]{:S(2)}) copy-start(bf16[128,1024]{1,0:T(8,128)(2,1)S(1)} %get-tuple-element.94) | copy-start | bytes 786436
  (2 other events, 3.2 us)
Sparse Core Ops, SparseCore 0:
  9.9 37.4 all-gather.4
  50.5 55.0 all-gather.8
  108.7 57.3 all-gather.6
where the time goes:
time: 507 us; the launch traced here: 506 us
  blocking collectives  227 us (45%)
  waiting for transfers between devices  167 us (33%)
  matrix products  39.4 us (8%)
  local copies, waits for them, and re-layouts  35.1 us (7%)
  between operations  16.4 us (3%)
  other arithmetic  15.5 us (3%)
    psum x1, blocking collectives, local(): lax.psum(norm_terms.astype(jnp.bfloat16), 'blk').astype(jnp.float32)  120 us
    pmax x1, blocking collectives, local(): greatest = lax.pmax(jnp.max(logits, axis=1), 'blk')  68.2 us
    all_gather x1, waiting for transfers between devices, local(): lax.all_gather(owner_prefix, 'blk', axis=0, tiled=True)  48.1 us
    all_gather x1, waiting for transfers between devices, local(): arrived = lax.all_gather(suffix_kv, 'blk', axis=0, tiled=True)  46.3 us
    all_to_all x1, blocking collectives, local(): lax.all_to_all(outgoing, 'blk', split_axis=0, concat_axis=0, tiled=True)  39.5 us
    all_gather x1, waiting for transfers between devices, local(): arrived = lax.all_gather(prefix_cache, 'grp', axis=0, tiled=True)  38.4 us
    all_to_all x1, waiting for transfers between devices, local(): lax.all_to_all(partial_value, 'blk', split_axis=0, concat_axis=0, tiled=T...  33.5 us
    dot_general x2, matrix products, attend_piece(): jnp.einsum('hqk,khd->hqd', probs_full.astype(jnp.bfloat16), value_heads,...  13.6 us
  transfers between devices with their start and end apart: 4, of which 4 were waited for; matrix products, arithmetic and copies ran while one was open for 4% of the time, Pallas kernels for 0%

commit v1 on v0

--- a/solution.py
+++ b/solution.py
@@ -8,6 +8,12 @@
 CAP = 40
 epsilon = 1e-06
 neg_big = -1e30
+
+
+def joined_along(tiles, dim):
+    tiles = jnp.moveaxis(tiles, 0, dim)
+    dims = tiles.shape
+    return tiles.reshape(*dims[:dim], dims[dim] * dims[dim + 1], *dims[dim + 2 :])
 
 
 def rms_scale(values, gain_vector):
@@ -143,7 +149,19 @@
     states = tuple((empty_state(one[0].shape[0], head_count, head_size) for one in query_sets))
     owner_id = owners[0]
     blank_prefix = jnp.zeros_like(prefix_cache[0])
-    arrived = lax.all_gather(prefix_cache, "grp", axis=0, tiled=True)
+    size = lax.axis_size("grp")
+    pairs = [(i, (i + 1) % size) for i in range(size)]
+    back = [(b, a) for a, b in pairs]
+    lower, upper = ([], [])
+    for step in range(size - 1):
+        if step % 2 == 0:
+            lower.append(lax.ppermute(lower[-1] if lower else prefix_cache, "grp", pairs))
+        else:
+            upper.append(lax.ppermute(upper[-1] if upper else prefix_cache, "grp", back))
+    blocks_2 = jnp.stack([*lower[::-1], prefix_cache, *upper])
+    shift = lax.axis_index("grp") - len(lower)
+    blocks_2 = blocks_2[(jnp.arange(size) - shift) % size]
+    arrived = joined_along(blocks_2, 0)
     first_row = jnp.int32(0)
     shard_count = arrived.shape[0]
     inside = (owner_id >= first_row) & (owner_id < first_row + shard_count)

time: 507 us -> 494 us (0.974)
  waiting for transfers between devices: 167 us -> 143 us
  starting transfers between devices: 4.83 us -> 15.8 us
    all_gather x1 -> x0, waiting for transfers between devices: 38.4 us -> none  [local(): arrived = lax.all_gather(prefix_cache, 'grp', axis=0, tiled=True)]
    ppermute x0 -> x7, waiting for transfers between devices: none -> 13.5 us  [the longest x4 13.4 us: local(): lax.ppermute(lower[-1] if lower else prefix_cache, 'grp', pairs)]
    ppermute x0 -> x7, starting transfers between devices: none -> 10.9 us  [the longest x3 8.3 us: local(): lax.ppermute(upper[-1] if upper else prefix_cache, 'grp', back)]
    another operation x3 -> x4, local copies, waits for them, and re-layouts: 11.5 us -> 11.5 us
  transfers between devices with their start and end apart: 4 -> 10, of which waited for: 4 -> 7; matrix products, arithmetic and copies ran while one was open for 4% -> 4% of each run, Pallas kernels for 0% -> 0%
where the time goes in v1:
time: 494 us
  blocking collectives  227 us (46%)
  waiting for transfers between devices  143 us (29%)
  local copies, waits for them, and re-layouts  38.9 us (8%)
  matrix products  38.5 us (8%)
  between operations  16.6 us (3%)
  starting transfers between devices  15.8 us (3%)
  other arithmetic  13.6 us (3%)
    psum x1, blocking collectives, local(): lax.psum(norm_terms.astype(jnp.bfloat16), 'blk').astype(jnp.float32)  120 us
    pmax x1, blocking collectives, local(): greatest = lax.pmax(jnp.max(logits, axis=1), 'blk')  68.2 us
    all_gather x1, waiting for transfers between devices, local(): lax.all_gather(owner_prefix, 'blk', axis=0, tiled=True)  49.2 us
    all_gather x1, waiting for transfers between devices, local(): arrived = lax.all_gather(suffix_kv, 'blk', axis=0, tiled=True)  46.3 us
    all_to_all x1, blocking collectives, local(): lax.all_to_all(outgoing, 'blk', split_axis=0, concat_axis=0, tiled=True)  39.5 us
    all_to_all x1, waiting for transfers between devices, local(): lax.all_to_all(partial_value, 'blk', split_axis=0, concat_axis=0, tiled=T...  33.5 us
    dot_general x2, matrix products, attend_piece(): jnp.einsum('hqk,khd->hqd', probs_full.astype(jnp.bfloat16), value_heads,...  13.6 us
    ppermute x4, waiting for transfers between devices, local(): lax.ppermute(lower[-1] if lower else prefix_cache, 'grp', pairs)  13.4 us
  transfers between devices with their start and end apart: 10, of which 7 were waited for; matrix products, arithmetic and copies ran while one was open for 4% of the time, Pallas kernels for 0%

profile of v1, /device:TPU:1, one launch (start us, length us, event | category | flops | bytes accessed | tf_op | source)
XLA Modules:
  0.0 493.7 jit_solution(16223565296967269438)
XLA Ops:
  7.2 2.5 collective-permute-start
  9.8 7.4 %collective-permute-done = bf16[1,64,1024]{2,1,0:T(8,128)(2,1)S(1)} collective-permute-done((bf16[1,64,1024]{2,1,0:T(8,128)(2,1)}, bf16[1,64,1024]{2,1,0:T(8,128)(2,1)S(1)}, u32[]{:S(2)}, u32[]{:S(2)}) %collective-permute-start) | collective-permute-done | bytes 131104 | tf_op jit(solution)/shard_map/ppermute | solution.py:158
  17.2 2.7 collective-permute-start.4
  22.2 2.9 collective-permute-start.5
  27.9 2.7 collective-permute-start.6
  43.7 49.2 %all-gather.7.cloned.1.call-done = bf16[1,2048,1024]{2,1,0:T(8,128)(2,1)} async-done(((bf16[1,64,1024]{2,1,0:T(8,128)(2,1)}), bf16[1,2048,1024]{2,1,0:T(8,128)(2,1)}) %all-gather.7.cloned.1.call-update) | async-done | bytes 4194320 | tf_op jit(solution)/shard_map/all_gather | solution.py:175
  92.9 3.8 fusion.71
  96.7 2.5 copy.47
  99.2 2.9 copy.46
  107.0 46.3 %all-gather.5.cloned.1.call-done = bf16[4096,1024]{1,0:T(8,128)(2,1)} async-done(((bf16[128,1024]{1,0:T(8,128)(2,1)}), bf16[4096,1024]{1,0:T(8,128)(2,1)}) %all-gather.5.cloned.1.call-update) | async-done | bytes 8388624 | tf_op jit(solution)/shard_map/all_gather | solution.py:181
  153.4 40.8 %conditional.1 = ((f32[8,128,64]{1,2,0:T(8,128)S(1)}, f32[8,128]{1,0:T(8,128)S(1)})) conditional(s32[]{:T(128)} %convert_element_type.95, (f32[8,128,64]{1,2,0:T(8,128)S(1)}, f32[8,128]{1,0:T(8,128)S(1)}) %tuple.16, (s32[128]{0:T(128)S(1)}, s32[4096,16]{0,1:T(8,128)S(1)}, s32[4096]{0:T(1024)S(1)}, s32[128]{0:T(128)S(1)}, ...), branch_computations={%region_5.6_spmd, %region_6.10_spmd} | conditional | flops 1121646592 | bytes 162767936 | solution.py:89
  153.6 11.3 %copy.49 = bf16[4096,1024]{0,1:T(8,128)(2,1)} copy(bf16[4096,1024]{1,0:T(8,128)(2,1)} %get-tuple-element.74) | data formatting | bytes 16777216 | tf_op jit(solution)/shard_map
  165.0 6.1 %fusion.70 = (bf16[4096,512]{0,1:T(8,128)(2,1)}, bf16[4096,512]{0,1:T(8,128)(2,1)}) fusion(bf16[4096,1024]{0,1:T(8,128)(2,1)} %copy.49), kind=kLoop, calls=%fused_computation.131 | loop fusion | bytes 16777216 | tf_op jit(solution)/shard_map/cond/branch_1_fun/slice | solution.py:57
  171.7 5.0 %fusion = (f32[8,128]{1,0:T(8,128)S(1)}, f32[8,128,4096]{2,1,0:T(8,128)S(1)}) fusion(pred[128,4096]{1,0:T(8,128)(4,1)S(1)} %compare_and_fusion, bf16[128,8,64]{0,2,1:T(8,128)(2,1)S(1)} %bitcast.116, bf16[4096,8,64]{0,2,1:T(8,128)(2,1)} %bitcast.104), kind=kOutput, calls=%fused_computation.5 | convolution fusion | flops 549452800 | bytes 21630976 | tf_op jit(solution)/shard_map/cond/branch_1_fun/qhd,khd->hqk/dot_general | solution.py:60
  176.7 4.8 fusion.1
  182.4 11.7 %fusion.6 = f32[8,128,64]{1,2,0:T(8,128)S(1)} fusion(bf16[4096,8,64]{0,2,1:T(8,128)(2,1)} %bitcast.109, f32[8,128,4096]{2,1,0:T(8,128)} %copy-done.2, f32[8,128]{1,0:T(8,128)S(1)} %max.12, pred[128,4096]{1,0:T(8,128)(4,1)S(1)} %compare_and_fusion, f32[8,128,64]{1,2,0:T(8,128)S(1)} %get-tuple-element.25, f32[8,128]{1,0:T(8,128)S(1)} %get-tuple-element.83), kind=kOutput, calls=%fused_computation.11 | convolution fusion | flops 553779200 | bytes 22028288 | tf_op jit(solution)/shard_map/cond/branch_1_fun/hqk,khd->hqd/dot_general | solution.py:72
  195.4 39.5 %all_to_all.10 = bf16[32,40,1024]{2,1,0:T(8,128)(2,1)S(1)} all-to-all(bf16[32,40,1024]{2,1,0:T(8,128)(2,1)S(1)} %bitcast.105), channel_id=1, replica_groups=mesh['grp'=8,'blk'=32] {'blk'}, dimensions={0} | all-to-all | bytes 5242880 | tf_op jit(solution)/shard_map/all_to_all | solution.py:199
  236.5 3.8 fusion.27
  240.3 9.7 %convolution_convert_fusion = bf16[1280,1024]{1,0:T(8,128)(2,1)} fusion(bf16[1,704,1024]{2,1,0:T(8,128)(2,1)S(1)} %copy-done.21, bf16[1280,1024]{1,0:T(8,128)(2,1)} %bitcast.112, f32[1280,704]{0,1:T(8,128)} %fusion.27, bf16[1,1024,704]{1,2,0:T(8,128)(2,1)} %param.32), kind=kOutput, calls=%fused_computation.26 | convolution fusion | flops 3701309440 | bytes 11730944 | tf_op jit(solution)/shard_map/dot_general | solution.py:205
  250.1 4.7 all-to-all-start.1
  254.9 33.5 %all-to-all-done.1 = bf16[32,40,1024]{2,1,0:T(8,128)(2,1)} async-done(((bf16[32,40,1024]{2,1,0:T(8,128)(2,1)}), bf16[32,40,1024]{2,1,0:T(8,128)(2,1)}, u32[]{:S(2)}, u32[]{:S(2)}) %all-to-all-start.1) | async-done | bytes 2621472 | tf_op jit(solution)/shard_map/all_to_all | solution.py:209
  288.4 2.4 convert_reduce_fusion
  296.0 119.8 %all-reduce = (bf16[16]{0:T(256)(128)(2,1)S(1)}, bf16[16,1024]{1,0:T(8,128)(2,1)S(1)}) all-reduce(bf16[16]{0:T(256)(128)(2,1)S(1)} %select_reduce_fusion, bf16[16,1024]{1,0:T(8,128)(2,1)S(1)} %convolution_convert_fusion.4), channel_id=1, replica_groups=mesh['grp'=8,'blk'=32] {'blk'}, use_global_device_ids=true, to_apply=%region_17.19 | all-reduce | flops 16400 | bytes 65600 | tf_op jit(solution)/shard_map/psum | solution.py:226
  418.6 68.2 %pmax.7 = f32[1,16]{1,0:T(1,128)} all-reduce(f32[1,16]{1,0:T(1,128)S(1)} %bitcast.121), channel_id=1, replica_groups=mesh['grp'=8,'blk'=32] {'blk'}, use_global_device_ids=true, to_apply=%region_20.22 | all-reduce | flops 16 | bytes 128 | tf_op jit(solution)/shard_map/pmax | solution.py:230
  (128 shorter events, 33.2 us)
Async XLA Ops:
  7.2 30.1 %copy-start = (bf16[1024,1024]{1,0:T(8,128)(2,1)S(1)}, bf16[1024,1024]{1,0:T(8,128)(2,1)}, u32[]{:S(2)}) copy-start(bf16[1024,1024]{1,0:T(8,128)(2,1)} %param.28) | copy-start | bytes 6291460
  7.2 29.9 %copy-start.5 = (bf16[1,128,1024]{2,1,0:T(8,128)(2,1)S(1)}, bf16[1,128,1024]{2,1,0:T(8,128)(2,1)}, u32[]{:S(2)}) copy-start(bf16[1,128,1024]{2,1,0:T(8,128)(2,1)} %param.20) | copy-start | bytes 786436
  7.2 30.1 %copy-start.11 = (f32[1024]{0:T(1024)S(1)}, f32[1024]{0:T(1024)}, u32[]{:S(2)}) copy-start(f32[1024]{0:T(1024)} %param.26) | copy-start | bytes 12292
  7.2 85.7 %all-gather.7.cloned.1.call-start = ((), (), s32[]{:S(2)}) async-start(), calls=%async_computation.3 | async-start | bytes 4325376 | tf_op jit(solution)/shard_map/all_gather | solution.py:175
  7.2 9.9 %collective-permute-start = (bf16[1,64,1024]{2,1,0:T(8,128)(2,1)}, bf16[1,64,1024]{2,1,0:T(8,128)(2,1)S(1)}, u32[]{:S(2)}, u32[]{:S(2)}) collective-permute-start(bf16[1,64,1024]{2,1,0:T(8,128)(2,1)} %param.23), channel_id=1, source_target_pairs={{0,32},{32,64},{64,96},{96,128},{128,160},{160,192},{192,224},{224... | collective-permute-start | bytes 393224 | tf_op jit(solution)/shard_map/ppermute | solution.py:158
  17.2 5.0 %collective-permute-start.1 = (bf16[1,64,1024]{2,1,0:T(8,128)(2,1)S(1)}, bf16[1,64,1024]{2,1,0:T(8,128)(2,1)S(1)}, u32[]{:S(2)}, u32[]{:S(2)}) collective-permute-start(bf16[1,64,1024]{2,1,0:T(8,128)(2,1)S(1)} %collective-permute-done), channel_id=1, source_target_pairs={{0,32},{32,64},{64,96},{96,128},{128,160},{160,192},{192,224},{224... | collective-permute-start | bytes 393224 | tf_op jit(solution)/shard_map/ppermute | solution.py:158
  17.2 5.0 %collective-permute-start.4 = (bf16[1,64,1024]{2,1,0:T(8,128)(2,1)}, bf16[1,64,1024]{2,1,0:T(8,128)(2,1)S(1)}, u32[]{:S(2)}, u32[]{:S(2)}) collective-permute-start(bf16[1,64,1024]{2,1,0:T(8,128)(2,1)} %param.23), channel_id=1, source_target_pairs={{32,0},{64,32},{96,64},{128,96},{160,128},{192,160},{224,192},{0,2... | collective-permute-start | bytes 393224 | tf_op jit(solution)/shard_map/ppermute | solution.py:160
  22.2 5.0 %collective-permute-start.2 = (bf16[1,64,1024]{2,1,0:T(8,128)(2,1)S(1)}, bf16[1,64,1024]{2,1,0:T(8,128)(2,1)S(1)}, u32[]{:S(2)}, u32[]{:S(2)}) collective-permute-start(bf16[1,64,1024]{2,1,0:T(8,128)(2,1)S(1)} %collective-permute-done.1), channel_id=1, source_target_pairs={{0,32},{32,64},{64,96},{96,128},{128,160},{160,192},{192,224},{224... | collective-permute-start | bytes 393224 | tf_op jit(solution)/shard_map/ppermute | solution.py:158
  22.2 5.7 %collective-permute-start.5 = (bf16[1,64,1024]{2,1,0:T(8,128)(2,1)S(1)}, bf16[1,64,1024]{2,1,0:T(8,128)(2,1)S(1)}, u32[]{:S(2)}, u32[]{:S(2)}) collective-permute-start(bf16[1,64,1024]{2,1,0:T(8,128)(2,1)S(1)} %collective-permute-done.4), channel_id=1, source_target_pairs={{32,0},{64,32},{96,64},{128,96},{160,128},{192,160},{224,192},{0,2... | collective-permute-start | bytes 393224 | tf_op jit(solution)/shard_map/ppermute | solution.py:160
  27.2 5.0 %collective-permute-start.3 = (bf16[1,64,1024]{2,1,0:T(8,128)(2,1)S(1)}, bf16[1,64,1024]{2,1,0:T(8,128)(2,1)S(1)}, u32[]{:S(2)}, u32[]{:S(2)}) collective-permute-start(bf16[1,64,1024]{2,1,0:T(8,128)(2,1)S(1)} %collective-permute-done.2), channel_id=1, source_target_pairs={{0,32},{32,64},{64,96},{96,128},{128,160},{160,192},{192,224},{224... | collective-permute-start | bytes 393224 | tf_op jit(solution)/shard_map/ppermute | solution.py:158
  27.9 5.4 %collective-permute-start.6 = (bf16[1,64,1024]{2,1,0:T(8,128)(2,1)S(1)}, bf16[1,64,1024]{2,1,0:T(8,128)(2,1)S(1)}, u32[]{:S(2)}, u32[]{:S(2)}) collective-permute-start(bf16[1,64,1024]{2,1,0:T(8,128)(2,1)S(1)} %collective-permute-done.5), channel_id=1, source_target_pairs={{32,0},{64,32},{96,64},{128,96},{160,128},{192,160},{224,192},{0,2... | collective-permute-start | bytes 393224 | tf_op jit(solution)/shard_map/ppermute | solution.py:160
  32.3 6.2 %copy-start.13 = (s32[1,128,2]{1,2,0:T(2,128)S(1)}, s32[1,128,2]{1,2,0:T(2,128)}, u32[]{:S(2)}) copy-start(s32[1,128,2]{1,2,0:T(2,128)} %param.24) | copy-start | bytes 3076
  32.3 7.9 %copy-start.15 = (s32[1,16]{1,0:T(1,128)S(1)}, s32[1,16]{1,0:T(1,128)}, u32[]{:S(2)}) copy-start(s32[1,16]{1,0:T(1,128)} %param.21) | copy-start | bytes 196
  36.9 116.5 %all-gather.5.cloned.1.call-start = ((), (), s32[]{:S(2)}) async-start(), calls=%async_computation.2 | async-start | bytes 8650752 | tf_op jit(solution)/shard_map/all_gather | solution.py:181
  105.2 48.2 %copy-start.17 = (s32[128]{0:T(128)S(1)}, s32[128]{0:T(128)}, u32[]{:S(2)}) copy-start(s32[128]{0:T(128)} %copy-done.16) | copy-start | bytes 1540
  105.2 48.2 %copy-start.19 = (s32[128]{0:T(128)S(1)}, s32[128]{0:T(128)}, u32[]{:S(2)}) copy-start(s32[128]{0:T(128)} %copy-done.18) | copy-start | bytes 1540
  153.4 40.8 %copy-start.9 = (bf16[512,1024]{1,0:T(8,128)(2,1)S(1)}, bf16[512,1024]{1,0:T(8,128)(2,1)}, u32[]{:S(2)}) copy-start(bf16[512,1024]{1,0:T(8,128)(2,1)} %param.29) | copy-start | bytes 3145732
  153.4 41.3 %copy-start.12 = (f32[1024]{0:T(1024)S(1)}, f32[1024]{0:T(1024)}, u32[]{:S(2)}) copy-start(f32[1024]{0:T(1024)} %param.30) | copy-start | bytes 12292
  176.7 5.7 %copy-start.2 = (f32[8,128,4096]{2,1,0:T(8,128)}, f32[8,128,4096]{2,1,0:T(8,128)S(1)}, u32[]{:S(2)}) copy-start(f32[8,128,4096]{2,1,0:T(8,128)S(1)} %get-tuple-element.89) | copy-start | bytes 50331652 | tf_op jit(solution)/shard_map/cond
  194.6 40.3 %copy-start.4 = (f32[128,1024]{1,0:T(8,128)}, f32[128,1024]{1,0:T(8,128)S(1)}, u32[]{:S(2)}) copy-start(f32[128,1024]{1,0:T(8,128)S(1)} %get-tuple-element.99) | copy-start | bytes 1572868
  195.1 41.4 %copy-start.20 = (bf16[1,1024,704]{1,2,0:T(8,128)(2,1)S(1)}, bf16[1,1024,704]{1,2,0:T(8,128)(2,1)}, u32[]{:S(2)}) copy-start(bf16[1,1024,704]{1,2,0:T(8,128)(2,1)} %param.31) | copy-start | bytes 4325380
  250.1 38.3 %all-to-all-start.1 = ((bf16[32,40,1024]{2,1,0:T(8,128)(2,1)}), bf16[32,40,1024]{2,1,0:T(8,128)(2,1)}, u32[]{:S(2)}, u32[]{:S(2)}) async-start(bf16[32,40,1024]{2,1,0:T(8,128)(2,1)} %bitcast.110), calls=%async_computation.1 | async-start | bytes 5242880 | tf_op jit(solution)/shard_map/all_to_all | solution.py:209
  292.3 194.5 %copy-start.1 = (bf16[1024,1024]{1,0:T(8,128)(2,1)S(1)}, bf16[1024,1024]{1,0:T(8,128)(2,1)}, u32[]{:S(2)}) copy-start(bf16[1024,1024]{1,0:T(8,128)(2,1)} %param.28) | copy-start | bytes 6291460
  295.6 191.2 %copy-start.10 = (bf16[128,1024]{1,0:T(8,128)(2,1)}, bf16[128,1024]{1,0:T(8,128)(2,1)S(1)}, u32[]{:S(2)}) copy-start(bf16[128,1024]{1,0:T(8,128)(2,1)S(1)} %get-tuple-element.85) | copy-start | bytes 786436
  (9 other events, 26.0 us)
Sparse Core Ops, SparseCore 0:
  37.0 55.8 all-gather.6
  96.0 57.3 all-gather.4
